TPU v7x, 32 devices: a whole 2x2x4 slice. The times are simulated.
32 devices in a mesh: pix: 16 (over z, y, core), frm: 2 (over x).
Axes of the slice: x: 2, y: 2, z: 4, core: 2. Of those that a mesh axis runs over, the one named last changes fastest.
Arguments:
- frames: bfloat16 [65536, 768], P('pix', 'frm'), may hold values from 0 to 6
- footprints: bfloat16 [65536, 192], P('pix'), may hold values from 0 to 0.024414062
- support: int32 [4096, 192], P('pix'), may hold values 0 or 1
- traces: float32 [1024, 768], P('pix', 'frm'), may hold values from 0 to 2
- block_order: int32 [16, 2], replicated, may hold values from 0 to 1, each once within a row
Outputs:
- refined: bfloat16 [65536, 192], P(('pix', 'frm'))
- updated: float32 [1024, 768], P('pix', 'frm')
Inputs may be any that keep to these rules, and one draw needn't show every extreme that they name: `block_order`: each row lists every block index of a slab once.
All inputs are finite; a program needn't handle non-finite values. No bound on the sum of `support` on one device may be relied on, other than what follows from the above.
Results may differ from a plain program's by a relative error of at most 0.0036.
Values may be sent and summed in bfloat16 or wider, within the bound.
A program may use at most 64 MiB of HBM per device.

v0:
```python
import jax
import jax.numpy as jnp
from jax import lax
from jax.sharding import PartitionSpec as P

BLOCK = 32
TILE = 16
highest = lax.Precision.HIGHEST


def from_behind(block, axis, distance):
    devices = range(lax.axis_size(axis))
    route = [(i - distance, i) for i in devices if i - distance in devices]
    return lax.ppermute(block, axis, route)


def window_mask(support, slab_id, owners, owner_width):
    expanded = jnp.repeat(support, TILE, axis=0).astype(jnp.float32)
    window_of = jnp.arange(3 * owner_width, dtype=jnp.int32) // owner_width
    usable = jnp.where(
        window_of == 0, slab_id > 0, jnp.where(window_of == 2, slab_id < owners - 1, True)
    )
    return expanded * usable.astype(jnp.float32)[None, :]


def trace_block(current, window, drive_rows, coupling, block_id, owner_width):
    row_start = block_id * BLOCK
    band_rows = lax.dynamic_slice_in_dim(coupling, row_start, BLOCK, 0)
    diagonal = jnp.diagonal(
        lax.dynamic_slice_in_dim(band_rows, 2 * owner_width + row_start, BLOCK, 1)
    )
    product = jnp.dot(band_rows, window, precision=highest)
    target = lax.dynamic_slice_in_dim(drive_rows, row_start, BLOCK, 0)
    before = lax.dynamic_slice_in_dim(current, row_start, BLOCK, 0)
    after = jnp.maximum(before + (target - product) / (diagonal[:, None] + 1.0), 0.0)
    return (after, row_start)


def trace_window(current):
    pieces = [from_behind(current, "pix", offset) for offset in (2, 1, -1, -2)]
    return jnp.concatenate([pieces[0], pieces[1], current, pieces[2], pieces[3]], axis=0)


def shards(frames, footprints, support, traces, block_order):
    owners = lax.axis_size("pix")
    slab_id = lax.axis_index("pix")
    owner_width = traces.shape[0]
    sweeps = owner_width // BLOCK
    keep = window_mask(support, slab_id, owners, owner_width)
    active = (footprints.astype(jnp.float32) * keep).astype(jnp.bfloat16)
    loads = jnp.einsum("pk,pt->kt", active, frames, preferred_element_type=jnp.float32)
    correlations = jnp.einsum("pk,pj->kj", active, active, preferred_element_type=jnp.float32)
    drive_rows = loads[owner_width : 2 * owner_width]
    coupling = jnp.pad(
        correlations[owner_width : 2 * owner_width], ((0, 0), (owner_width, owner_width))
    )
    for offset, window_id in ((-1, 0), (1, 2)):
        lower = window_id * owner_width
        arrived = from_behind(
            (loads[lower : lower + owner_width], correlations[lower : lower + owner_width]),
            "pix",
            offset,
        )
        drive_rows = drive_rows + arrived[0]
        if offset == -1:
            coupling = coupling + jnp.pad(arrived[1], ((0, 0), (2 * owner_width, 0)))
        else:
            coupling = coupling + jnp.pad(arrived[1], ((0, 0), (0, 2 * owner_width)))
    current = traces
    for step in range(sweeps):
        window = trace_window(current)
        after, row_start = trace_block(
            current, window, drive_rows, coupling, block_order[slab_id, step], owner_width
        )
        current = lax.dynamic_update_slice_in_dim(current, after, row_start, 0)
    beside = [from_behind(current, "pix", offset) for offset in (1, -1)]
    near_rows = jnp.concatenate([beside[0], current, beside[1]], axis=0)
    rounded = near_rows.astype(jnp.bfloat16)
    shares = lax.axis_size("frm")
    share_rows = footprints.shape[0] // shares
    row_begin = lax.axis_index("frm") * share_rows
    pixel_rows = lax.all_to_all(frames, "frm", split_axis=0, concat_axis=1, tiled=True)
    all_traces = lax.all_gather(rounded, "frm", axis=1, tiled=True)
    mixing = jnp.einsum("pt,kt->pk", pixel_rows, all_traces, preferred_element_type=jnp.float32)
    gram = jnp.einsum("kt,jt->kj", all_traces, all_traces, preferred_element_type=jnp.float32)
    shaped = lax.dynamic_slice_in_dim(active, row_begin, share_rows, 0).astype(jnp.float32)
    keep_rows = lax.dynamic_slice_in_dim(keep, row_begin, share_rows, 0)
    for step in range(sweeps):
        slab_near = jnp.clip(slab_id - 1 + jnp.arange(3, dtype=jnp.int32), 0, owners - 1)
        picked = block_order[slab_near, step]
        columns = (
            jnp.arange(3, dtype=jnp.int32)[:, None] * owner_width
            + picked[:, None] * BLOCK
            + jnp.arange(BLOCK, dtype=jnp.int32)[None, :]
        ).reshape(-1)
        gram_cols = jnp.take(gram, columns, axis=1)
        diagonal = jnp.diagonal(jnp.take(gram_cols, columns, axis=0))
        before = jnp.take(shaped, columns, axis=1)
        target = jnp.take(mixing, columns, axis=1)
        keep_cols = jnp.take(keep_rows, columns, axis=1)
        product = jnp.dot(shaped, gram_cols, precision=highest)
        after = (
            jnp.maximum(before + (target - product) / (diagonal[None, :] + 1.0), 0.0) * keep_cols
        )
        shaped = shaped.at[:, columns].set(after)
    return (shaped.astype(jnp.bfloat16), current)


def solution(mesh):
    in_specs = (P("pix", "frm"), P("pix", None), P("pix", None), P("pix", "frm"), P())
    out_specs = (P(("pix", "frm"), None), P("pix", "frm"))
    return jax.shard_map(shards, mesh=mesh, in_specs=in_specs, out_specs=out_specs, check_vma=False)
```

profile of v0, /device:TPU:10, one launch (start us, length us, event | category | flops | bytes accessed | tf_op | source)
XLA Modules:
  0.0 125.7 jit_solution(3920926233574790244)
XLA Ops:
  0.6 0.9 copy.38
  1.5 2.7 %collective-permute-start.6 = (f32[64,384]{1,0:T(8,128)S(1)}, f32[64,384]{1,0:T(8,128)}, u32[]{:S(2)}, u32[]{:S(2)}) collective-permute-start(f32[64,384]{1,0:T(8,128)S(1)} %copy.38), channel_id=1, source_target_pairs={{2,0},{4,2},{6,4},{8,6},{10,8},{12,10},{14,12},{16,14},{18,16},{20... | collective-permute-start | bytes 294920 | tf_op jit(solution)/shard_map/ppermute | solution.py:14
  4.3 1.9 %collective-permute-start.5 = (f32[64,384]{1,0:T(8,128)S(1)}, f32[64,384]{1,0:T(8,128)}, u32[]{:S(2)}, u32[]{:S(2)}) collective-permute-start(f32[64,384]{1,0:T(8,128)S(1)} %copy.38), channel_id=1, source_target_pairs={{0,2},{2,4},{4,6},{6,8},{8,10},{10,12},{12,14},{14,16},{16,18},{18... | collective-permute-start | bytes 294920 | tf_op jit(solution)/shard_map/ppermute | solution.py:14
  6.2 3.1 %collective-permute-start.4 = (f32[64,384]{1,0:T(8,128)S(1)}, f32[64,384]{1,0:T(8,128)}, u32[]{:S(2)}, u32[]{:S(2)}) collective-permute-start(f32[64,384]{1,0:T(8,128)S(1)} %copy.38), channel_id=1, source_target_pairs={{0,4},{2,6},{4,8},{6,10},{8,12},{10,14},{12,16},{14,18},{16,20},{1... | collective-permute-start | bytes 294920 | tf_op jit(solution)/shard_map/ppermute | solution.py:14
  9.3 5.9 %all-to-all-start = ((bf16[2,2048,384]{2,1,0:T(8,128)(2,1)}), bf16[2,2048,384]{2,1,0:T(8,128)(2,1)}, u32[]{:S(2)}, u32[]{:S(2)}) async-start(bf16[2,2048,384]{2,1,0:T(8,128)(2,1)} %bitcast.56), calls=%async_computation | async-start | bytes 6291456 | tf_op jit(solution)/shard_map/all_to_all | solution.py:82
  15.3 2.3 %broadcast_in_dim.69 = f32[256,16,192]{2,1,0:T(8,128)} broadcast(f32[256,192]{1,0:T(8,128)S(1)} %copy.17), dimensions={0,2} | broadcast | bytes 3342336 | tf_op jit(solution)/shard_map/broadcast_in_dim | solution.py:18
  17.6 5.4 %copy.18 = f32[4096,192]{0,1:T(8,128)} copy(f32[4096,192]{1,0:T(8,128)} %bitcast.55) | data formatting | bytes 6291456 | tf_op jit(solution)/shard_map/convert_element_type | solution.py:18
  23.1 4.4 %multiply_convert_fusion = (bf16[4096,192]{0,1:T(8,128)(2,1)S(1)}, f32[4096,192]{0,1:T(8,128)}) fusion(bf16[4096,192]{0,1:T(8,128)(2,1)S(1)} %copy-done.5, f32[4096,192]{0,1:T(8,128)} %copy.18, f32[192]{0:T(256)S(1)} %select_convert_fusion), kind=kLoop, calls=%fused_computation.18 | loop fusion | flops 3145728 | bytes 9437952 | tf_op jit(solution)/shard_map/convert_element_type | solution.py:50
  27.5 0.6 fusion.33
  28.1 0.7 fusion.29
  28.8 3.3 %collective-permute-start.3 = (f32[64,192]{1,0:T(8,128)}, f32[64,192]{1,0:T(8,128)}, u32[]{:S(2)}, u32[]{:S(2)}) collective-permute-start(f32[64,192]{1,0:T(8,128)} %get-tuple-element.10), channel_id=1, source_target_pairs={{0,2},{2,4},{4,6},{6,8},{8,10},{10,12},{12,14},{14,16},{16,18},{18... | collective-permute-start | bytes 147464 | tf_op jit(solution)/shard_map/ppermute | solution.py:14
  32.1 3.1 %collective-permute-start.2 = (f32[64,192]{1,0:T(8,128)}, f32[64,192]{1,0:T(8,128)}, u32[]{:S(2)}, u32[]{:S(2)}) collective-permute-start(f32[64,192]{1,0:T(8,128)} %get-tuple-element.11), channel_id=1, source_target_pairs={{2,0},{4,2},{6,4},{8,6},{10,8},{12,10},{14,12},{16,14},{18,16},{20... | collective-permute-start | bytes 147464 | tf_op jit(solution)/shard_map/ppermute | solution.py:14
  35.3 0.7 gather_fusion.4
  36.2 0.7 gather_fusion
  37.1 0.5 compare_select_fusion
  37.6 0.6 compare_select_fusion.1
  38.2 0.5 compare_and_fusion
  38.7 2.9 %fusion.32 = f32[192,384]{1,0:T(8,128)S(1)} fusion(bf16[4096,192]{0,1:T(8,128)(2,1)S(1)} %get-tuple-element.4, bf16[4096,384]{1,0:T(8,128)(2,1)} %param.11), kind=kOutput, calls=%fused_computation.100 | convolution fusion | flops 603979776 | bytes 5013504 | tf_op jit(solution)/shard_map/pk,pt->kt/dot_general | solution.py:51
  41.8 1.5 %constant_dynamic-slice_fusion.1 = f32[2048,192]{0,1:T(8,128)S(1)} fusion(f32[4096,192]{0,1:T(8,128)} %get-tuple-element.6, s32[]{:T(128)S(6)} %select_n.126), kind=kLoop, calls=%fused_computation.70 | loop fusion | bytes 3145732 | tf_op jit(solution)/shard_map/dynamic_slice | solution.py:87
  43.3 0.7 fusion.28
  44.0 0.6 fusion.25
  44.6 0.7 constant_dynamic-slice_fusion.2
  46.5 2.8 %collective-permute-start.7 = (f32[64,384]{1,0:T(8,128)S(1)}, f32[64,384]{1,0:T(8,128)S(1)}, u32[]{:S(2)}, u32[]{:S(2)}) collective-permute-start(f32[64,384]{1,0:T(8,128)S(1)} %copy.38), channel_id=1, source_target_pairs={{4,0},{6,2},{8,4},{10,6},{12,8},{14,10},{16,12},{18,14},{20,16},{2... | collective-permute-start | bytes 294920 | tf_op jit(solution)/shard_map/ppermute | solution.py:14
  49.4 2.7 %collective-permute-start = (f32[64,384]{1,0:T(8,128)}, f32[64,384]{1,0:T(8,128)}, u32[]{:S(2)}, u32[]{:S(2)}) collective-permute-start(f32[64,384]{1,0:T(8,128)} %get-tuple-element.7), channel_id=1, source_target_pairs={{2,0},{4,2},{6,4},{8,6},{10,8},{12,10},{14,12},{16,14},{18,16},{20... | collective-permute-start | bytes 294920 | tf_op jit(solution)/shard_map/ppermute | solution.py:14
  52.1 1.0 pad_add_fusion
  53.2 0.7 gather_fusion.1
  53.9 0.7 gather_fusion.2
  54.7 1.9 %collective-permute-start.1 = (f32[64,384]{1,0:T(8,128)}, f32[64,384]{1,0:T(8,128)S(1)}, u32[]{:S(2)}, u32[]{:S(2)}) collective-permute-start(f32[64,384]{1,0:T(8,128)} %get-tuple-element.8), channel_id=1, source_target_pairs={{0,2},{2,4},{4,6},{6,8},{8,10},{10,12},{12,14},{14,16},{16,18},{18... | collective-permute-start | bytes 294920 | tf_op jit(solution)/shard_map/ppermute | solution.py:14
  56.6 0.9 constant_dynamic-update-slice_fusion.4
  57.5 0.9 constant_dynamic-update-slice_fusion.3
  58.4 0.9 constant_dynamic-update-slice_fusion.1
  59.3 2.4 %collective-permute-done.1 = f32[64,384]{1,0:T(8,128)S(1)} collective-permute-done((f32[64,384]{1,0:T(8,128)}, f32[64,384]{1,0:T(8,128)S(1)}, u32[]{:S(2)}, u32[]{:S(2)}) %collective-permute-start.1) | collective-permute-done | bytes 98336 | tf_op jit(solution)/shard_map/ppermute | solution.py:14
  61.7 1.0 fusion.11
  62.7 0.4 maximum_dynamic-update-slice_fusion.1
  63.0 1.9 %collective-permute-start.8 = (f32[64,384]{1,0:T(8,128)S(1)}, f32[64,384]{1,0:T(8,128)S(1)}, u32[]{:S(2)}, u32[]{:S(2)}) collective-permute-start(f32[64,384]{1,0:T(8,128)S(1)} %maximum_dynamic-update-slice_fusion.1), channel_id=1, source_target_pairs={{0,4},{2,6},{4,8},{6,10},{8,12},{10,14},{12,16},{14,18},{16,20},{1... | collective-permute-start | bytes 294920 | tf_op jit(solution)/shard_map/ppermute | solution.py:14
  65.0 4.8 %collective-permute-start.11 = (f32[64,384]{1,0:T(8,128)S(1)}, f32[64,384]{1,0:T(8,128)S(1)}, u32[]{:S(2)}, u32[]{:S(2)}) collective-permute-start(f32[64,384]{1,0:T(8,128)S(1)} %maximum_dynamic-update-slice_fusion.1), channel_id=1, source_target_pairs={{4,0},{6,2},{8,4},{10,6},{12,8},{14,10},{16,12},{18,14},{20,16},{2... | collective-permute-start | bytes 294920 | tf_op jit(solution)/shard_map/ppermute | solution.py:14
  69.8 1.9 %collective-permute-start.10 = (f32[64,384]{1,0:T(8,128)S(1)}, f32[64,384]{1,0:T(8,128)S(1)}, u32[]{:S(2)}, u32[]{:S(2)}) collective-permute-start(f32[64,384]{1,0:T(8,128)S(1)} %maximum_dynamic-update-slice_fusion.1), channel_id=1, source_target_pairs={{2,0},{4,2},{6,4},{8,6},{10,8},{12,10},{14,12},{16,14},{18,16},{20... | collective-permute-start | bytes 294920 | tf_op jit(solution)/shard_map/ppermute | solution.py:14
  71.7 2.4 %collective-permute-start.9 = (f32[64,384]{1,0:T(8,128)S(1)}, f32[64,384]{1,0:T(8,128)S(1)}, u32[]{:S(2)}, u32[]{:S(2)}) collective-permute-start(f32[64,384]{1,0:T(8,128)S(1)} %maximum_dynamic-update-slice_fusion.1), channel_id=1, source_target_pairs={{0,2},{2,4},{4,6},{6,8},{8,10},{10,12},{12,14},{14,16},{16,18},{18... | collective-permute-start | bytes 294920 | tf_op jit(solution)/shard_map/ppermute | solution.py:14
  74.2 4.4 %collective-permute-done.9 = f32[64,384]{1,0:T(8,128)S(1)} collective-permute-done((f32[64,384]{1,0:T(8,128)S(1)}, f32[64,384]{1,0:T(8,128)S(1)}, u32[]{:S(2)}, u32[]{:S(2)}) %collective-permute-start.9) | collective-permute-done | bytes 98336 | tf_op jit(solution)/shard_map/ppermute | solution.py:14
  78.7 0.4 maximum_dynamic-update-slice_fusion
  79.1 1.9 %collective-permute-start.13 = (bf16[64,384]{1,0:T(8,128)(2,1)S(1)}, bf16[64,384]{1,0:T(8,128)(2,1)S(1)}, u32[]{:S(2)}, u32[]{:S(2)}) collective-permute-start(bf16[64,384]{1,0:T(8,128)(2,1)S(1)} %convert.27), channel_id=1, source_target_pairs={{2,0},{4,2},{6,4},{8,6},{10,8},{12,10},{14,12},{16,14},{18,16},{20... | collective-permute-start | bytes 147464 | tf_op jit(solution)/shard_map/ppermute | solution.py:14
  81.0 2.4 %collective-permute-start.12 = (bf16[64,384]{1,0:T(8,128)(2,1)S(1)}, bf16[64,384]{1,0:T(8,128)(2,1)S(1)}, u32[]{:S(2)}, u32[]{:S(2)}) collective-permute-start(bf16[64,384]{1,0:T(8,128)(2,1)S(1)} %convert.27), channel_id=1, source_target_pairs={{0,2},{2,4},{4,6},{6,8},{8,10},{10,12},{12,14},{14,16},{16,18},{18... | collective-permute-start | bytes 147464 | tf_op jit(solution)/shard_map/ppermute | solution.py:14
  83.4 1.7 %gather_fusion.15 = f32[96,2048]{1,0:T(8,128)} fusion(f32[2048,192]{0,1:T(8,128)S(1)} %constant_dynamic-slice_fusion.1, s32[1024]{0:T(1024)S(1)} %get-tuple-element.23), kind=kCustom, calls=%fused_computation.7.clone | custom fusion | bytes 1573248 | tf_op jit(solution)/shard_map/jit(_take)/gather | solution.py:100
  85.2 1.7 %gather_fusion.10 = f32[96,2048]{1,0:T(8,128)} fusion(f32[2048,192]{0,1:T(8,128)S(1)} %constant_dynamic-slice_fusion.1, s32[1024]{0:T(1024)S(1)} %get-tuple-element.24), kind=kCustom, calls=%fused_computation.4.clone | custom fusion | bytes 1573248 | tf_op jit(solution)/shard_map/jit(_take)/gather | solution.py:100
  86.9 1.8 %gather_fusion.6 = f32[96,2048]{1,0:T(8,128)} fusion(f32[2048,192]{0,1:T(8,128)S(1)} %dynamic-slice_convert_fusion, s32[1024]{0:T(1024)S(1)} %get-tuple-element.24), kind=kCustom, calls=%fused_computation.clone | custom fusion | bytes 1573248 | tf_op jit(solution)/shard_map/jit(_take)/gather | solution.py:98
  88.7 6.4 %all_gather.3 = bf16[192,768]{1,0:T(8,128)(2,1)S(1)} all-gather(bf16[192,384]{1,0:T(8,128)(2,1)S(1)} %pad_maximum_fusion), channel_id=1, replica_groups=mesh['pix'=16,'frm'=2] {'frm'}, dimensions={1}, use_global_device_ids=true | all-gather | bytes 442368 | tf_op jit(solution)/shard_map/all_gather | solution.py:83
  95.4 0.7 gather_fusion.8
  96.2 0.7 gather_fusion.13
  97.0 0.6 gather_fusion.14
  97.9 0.6 gather_fusion.9
  98.6 1.2 gather_fusion.5
  99.9 1.2 gather_fusion.3
  101.2 0.5 broadcast_add_fusion
  101.7 0.6 broadcast_add_fusion.1
  102.2 4.7 %copy.19 = bf16[2048,2,384]{0,2,1:T(8,128)(2,1)} copy(bf16[2048,2,384]{2,0,1:T(8,128)(2,1)} %bitcast.8) | data formatting | bytes 6291456 | tf_op jit(solution)/shard_map/all_to_all | solution.py:82
  106.9 2.7 %convolution_bitcast_fusion = f32[2048,192]{0,1:T(8,128)S(1)} fusion(bf16[192,768]{1,0:T(8,128)(2,1)S(1)} %all_gather.3, bf16[2048,768]{0,1:T(8,128)(2,1)} %bitcast.57), kind=kOutput, calls=%fused_computation.19 | convolution fusion | flops 603979776 | bytes 5013504 | tf_op jit(solution)/shard_map/pt,kt->pk/dot_general | solution.py:84
  109.6 1.8 %gather_fusion.12 = f32[96,2048]{1,0:T(8,128)} fusion(f32[2048,192]{0,1:T(8,128)S(1)} %convolution_bitcast_fusion, s32[1024]{0:T(1024)S(1)} %get-tuple-element.23), kind=kCustom, calls=%fused_computation.6.clone | custom fusion | bytes 1573248 | tf_op jit(solution)/shard_map/jit(_take)/gather | solution.py:99
  111.5 1.7 %gather_fusion.7 = f32[96,2048]{1,0:T(8,128)} fusion(f32[2048,192]{0,1:T(8,128)S(1)} %convolution_bitcast_fusion, s32[1024]{0:T(1024)S(1)} %get-tuple-element.24), kind=kCustom, calls=%fused_computation.3.clone | custom fusion | bytes 1573248 | tf_op jit(solution)/shard_map/jit(_take)/gather | solution.py:99
  113.2 2.5 %fusion.9 = f32[96,2048]{1,0:T(8,128)S(1)} fusion(f32[96,2048]{1,0:T(8,128)} %gather_fusion.10, f32[96,2048]{1,0:T(8,128)} %gather_fusion.7, f32[96,2048]{1,0:T(8,128)} %gather_fusion.6, bf16[4096,192]{0,1:T(8,128)(2,1)} %copy-done.1, s32[]{:T(128)S(6)} %select_n.126, f32[96]{0:T(128)S(1)} %copy-done.17, pred[96]{0:T(512)(128)(4,1)S(1)} %copy-done.11, ...), kind=kOutput, calls=%fused_computation.31 | convolution fusion | flops 454576128 | bytes 4032004 | tf_op jit(solution)/shard_map/dot_general | solution.py:101
  115.8 1.7 %scatter_fusion = f32[2048,192]{0,1:T(8,128)S(1)} fusion(f32[2048,192]{0,1:T(8,128)S(1)} %dynamic-slice_convert_fusion, s32[96]{0:T(128)S(1)} %copy-done.13, f32[96,2048]{1,0:T(8,128)S(1)} %fusion.9), kind=kCustom, calls=%fused_computation.16 | custom fusion | bytes 2359680 | tf_op jit(solution)/shard_map/scatter | solution.py:105
  117.4 1.7 %gather_fusion.11 = f32[96,2048]{1,0:T(8,128)} fusion(f32[2048,192]{0,1:T(8,128)S(1)} %scatter_fusion, s32[1024]{0:T(1024)S(1)} %get-tuple-element.23), kind=kCustom, calls=%fused_computation.5.clone | custom fusion | bytes 1573248 | tf_op jit(solution)/shard_map/jit(_take)/gather | solution.py:98
  119.2 3.2 %fusion.5 = f32[96,2048]{1,0:T(8,128)} fusion(f32[2048,192]{0,1:T(8,128)S(1)} %scatter_fusion, f32[96,2048]{1,0:T(8,128)S(1)} %copy-done.2, f32[96,2048]{1,0:T(8,128)S(1)} %copy-done.3, f32[96,2048]{1,0:T(8,128)} %gather_fusion.11, f32[96]{0:T(128)S(1)} %copy-done.16, pred[96]{0:T(512)(128)(4,1)S(1)} %get-tuple-element.19, f32[96,192]{1,0:T(8,128)S(1)} %gather_fusion.13), kind=kOutput, calls=%fused_computation.27 | convolution fusion | flops 454576128 | bytes 4792800 | tf_op jit(solution)/shard_map/dot_general | solution.py:101
  122.4 2.2 %scatter_fusion.1 = f32[2048,192]{0,1:T(8,128)S(1)} fusion(f32[2048,192]{0,1:T(8,128)S(1)} %scatter_fusion, s32[96]{0:T(128)S(1)} %copy-done.12, f32[96,2048]{1,0:T(8,128)} %fusion.5), kind=kCustom, calls=%fused_computation.17 | custom fusion | bytes 2359680 | tf_op jit(solution)/shard_map/scatter | solution.py:105
  124.7 1.0 convert_element_type.39
  (85 shorter events, 1.9 us)
Async XLA Ops:
  1.5 56.9 %collective-permute-start.6 = (f32[64,384]{1,0:T(8,128)S(1)}, f32[64,384]{1,0:T(8,128)}, u32[]{:S(2)}, u32[]{:S(2)}) collective-permute-start(f32[64,384]{1,0:T(8,128)S(1)} %copy.38), channel_id=1, source_target_pairs={{2,0},{4,2},{6,4},{8,6},{10,8},{12,10},{14,12},{16,14},{18,16},{20... | collective-permute-start | bytes 294920 | tf_op jit(solution)/shard_map/ppermute | solution.py:14
  4.3 53.2 %collective-permute-start.5 = (f32[64,384]{1,0:T(8,128)S(1)}, f32[64,384]{1,0:T(8,128)}, u32[]{:S(2)}, u32[]{:S(2)}) collective-permute-start(f32[64,384]{1,0:T(8,128)S(1)} %copy.38), channel_id=1, source_target_pairs={{0,2},{2,4},{4,6},{6,8},{8,10},{10,12},{12,14},{14,16},{16,18},{18... | collective-permute-start | bytes 294920 | tf_op jit(solution)/shard_map/ppermute | solution.py:14
  6.2 48.5 %collective-permute-start.4 = (f32[64,384]{1,0:T(8,128)S(1)}, f32[64,384]{1,0:T(8,128)}, u32[]{:S(2)}, u32[]{:S(2)}) collective-permute-start(f32[64,384]{1,0:T(8,128)S(1)} %copy.38), channel_id=1, source_target_pairs={{0,4},{2,6},{4,8},{6,10},{8,12},{10,14},{12,16},{14,18},{16,20},{1... | collective-permute-start | bytes 294920 | tf_op jit(solution)/shard_map/ppermute | solution.py:14
  9.3 5.9 %copy-start.9 = (s32[256,192]{0,1:T(8,128)S(1)}, s32[256,192]{0,1:T(8,128)}, u32[]{:S(2)}) copy-start(s32[256,192]{0,1:T(8,128)} %param.13) | copy-start | bytes 589828
  9.3 92.9 %all-to-all-start = ((bf16[2,2048,384]{2,1,0:T(8,128)(2,1)}), bf16[2,2048,384]{2,1,0:T(8,128)(2,1)}, u32[]{:S(2)}, u32[]{:S(2)}) async-start(bf16[2,2048,384]{2,1,0:T(8,128)(2,1)} %bitcast.56), calls=%async_computation | async-start | bytes 6291456 | tf_op jit(solution)/shard_map/all_to_all | solution.py:82
  17.6 5.5 %copy-start.5 = (bf16[4096,192]{0,1:T(8,128)(2,1)S(1)}, bf16[4096,192]{0,1:T(8,128)(2,1)}, u32[]{:S(2)}) copy-start(bf16[4096,192]{0,1:T(8,128)(2,1)} %param.12) | copy-start | bytes 4718596
  27.5 14.1 %copy-start.1 = (bf16[4096,192]{0,1:T(8,128)(2,1)}, bf16[4096,192]{0,1:T(8,128)(2,1)S(1)}, u32[]{:S(2)}) copy-start(bf16[4096,192]{0,1:T(8,128)(2,1)S(1)} %get-tuple-element.4) | copy-start | bytes 4718596
  27.5 7.8 %copy-start = (s32[16,2]{0,1:T(2,128)S(1)}, s32[16,2]{0,1:T(2,128)}, u32[]{:S(2)}) copy-start(s32[16,2]{0,1:T(2,128)} %param.15) | copy-start | bytes 388
  28.8 17.8 %collective-permute-start.3 = (f32[64,192]{1,0:T(8,128)}, f32[64,192]{1,0:T(8,128)}, u32[]{:S(2)}, u32[]{:S(2)}) collective-permute-start(f32[64,192]{1,0:T(8,128)} %get-tuple-element.10), channel_id=1, source_target_pairs={{0,2},{2,4},{4,6},{6,8},{8,10},{10,12},{12,14},{14,16},{16,18},{18... | collective-permute-start | bytes 147464 | tf_op jit(solution)/shard_map/ppermute | solution.py:14
  32.1 17.3 %collective-permute-start.2 = (f32[64,192]{1,0:T(8,128)}, f32[64,192]{1,0:T(8,128)}, u32[]{:S(2)}, u32[]{:S(2)}) collective-permute-start(f32[64,192]{1,0:T(8,128)} %get-tuple-element.11), channel_id=1, source_target_pairs={{2,0},{4,2},{6,4},{8,6},{10,8},{12,10},{14,12},{16,14},{18,16},{20... | collective-permute-start | bytes 147464 | tf_op jit(solution)/shard_map/ppermute | solution.py:14
  41.6 1.7 %copy-start.6 = (f32[192,384]{1,0:T(8,128)}, f32[192,384]{1,0:T(8,128)S(1)}, u32[]{:S(2)}) copy-start(f32[192,384]{1,0:T(8,128)S(1)} %fusion.32) | copy-start | bytes 884740
  41.8 2.8 %copy-start.14 = (s32[96]{0:T(128)S(1)}, s32[96]{0:T(128)}, u32[]{:S(2)}) copy-start(s32[96]{0:T(128)} %compare_select_fusion) | copy-start | bytes 1156
  41.8 2.8 %copy-start.15 = (s32[96]{0:T(128)S(1)}, s32[96]{0:T(128)}, u32[]{:S(2)}) copy-start(s32[96]{0:T(128)} %compare_select_fusion.1) | copy-start | bytes 1156
  46.5 12.8 %collective-permute-start.7 = (f32[64,384]{1,0:T(8,128)S(1)}, f32[64,384]{1,0:T(8,128)S(1)}, u32[]{:S(2)}, u32[]{:S(2)}) collective-permute-start(f32[64,384]{1,0:T(8,128)S(1)} %copy.38), channel_id=1, source_target_pairs={{4,0},{6,2},{8,4},{10,6},{12,8},{14,10},{16,12},{18,14},{20,16},{2... | collective-permute-start | bytes 294920 | tf_op jit(solution)/shard_map/ppermute | solution.py:14
  49.4 10.0 %collective-permute-start = (f32[64,384]{1,0:T(8,128)}, f32[64,384]{1,0:T(8,128)}, u32[]{:S(2)}, u32[]{:S(2)}) collective-permute-start(f32[64,384]{1,0:T(8,128)} %get-tuple-element.7), channel_id=1, source_target_pairs={{2,0},{4,2},{6,4},{8,6},{10,8},{12,10},{14,12},{16,14},{18,16},{20... | collective-permute-start | bytes 294920 | tf_op jit(solution)/shard_map/ppermute | solution.py:14
  54.7 7.0 %collective-permute-start.1 = (f32[64,384]{1,0:T(8,128)}, f32[64,384]{1,0:T(8,128)S(1)}, u32[]{:S(2)}, u32[]{:S(2)}) collective-permute-start(f32[64,384]{1,0:T(8,128)} %get-tuple-element.8), channel_id=1, source_target_pairs={{0,2},{2,4},{4,6},{6,8},{8,10},{10,12},{12,14},{14,16},{16,18},{18... | collective-permute-start | bytes 294920 | tf_op jit(solution)/shard_map/ppermute | solution.py:14
  63.0 11.1 %collective-permute-start.8 = (f32[64,384]{1,0:T(8,128)S(1)}, f32[64,384]{1,0:T(8,128)S(1)}, u32[]{:S(2)}, u32[]{:S(2)}) collective-permute-start(f32[64,384]{1,0:T(8,128)S(1)} %maximum_dynamic-update-slice_fusion.1), channel_id=1, source_target_pairs={{0,4},{2,6},{4,8},{6,10},{8,12},{10,14},{12,16},{14,18},{16,20},{1... | collective-permute-start | bytes 294920 | tf_op jit(solution)/shard_map/ppermute | solution.py:14
  65.0 13.7 %collective-permute-start.11 = (f32[64,384]{1,0:T(8,128)S(1)}, f32[64,384]{1,0:T(8,128)S(1)}, u32[]{:S(2)}, u32[]{:S(2)}) collective-permute-start(f32[64,384]{1,0:T(8,128)S(1)} %maximum_dynamic-update-slice_fusion.1), channel_id=1, source_target_pairs={{4,0},{6,2},{8,4},{10,6},{12,8},{14,10},{16,12},{18,14},{20,16},{2... | collective-permute-start | bytes 294920 | tf_op jit(solution)/shard_map/ppermute | solution.py:14
  69.8 8.8 %collective-permute-start.10 = (f32[64,384]{1,0:T(8,128)S(1)}, f32[64,384]{1,0:T(8,128)S(1)}, u32[]{:S(2)}, u32[]{:S(2)}) collective-permute-start(f32[64,384]{1,0:T(8,128)S(1)} %maximum_dynamic-update-slice_fusion.1), channel_id=1, source_target_pairs={{2,0},{4,2},{6,4},{8,6},{10,8},{12,10},{14,12},{16,14},{18,16},{20... | collective-permute-start | bytes 294920 | tf_op jit(solution)/shard_map/ppermute | solution.py:14
  71.7 6.8 %collective-permute-start.9 = (f32[64,384]{1,0:T(8,128)S(1)}, f32[64,384]{1,0:T(8,128)S(1)}, u32[]{:S(2)}, u32[]{:S(2)}) collective-permute-start(f32[64,384]{1,0:T(8,128)S(1)} %maximum_dynamic-update-slice_fusion.1), channel_id=1, source_target_pairs={{0,2},{2,4},{4,6},{6,8},{8,10},{10,12},{12,14},{14,16},{16,18},{18... | collective-permute-start | bytes 294920 | tf_op jit(solution)/shard_map/ppermute | solution.py:14
  79.1 6.1 %copy-start.4 = (f32[64,384]{1,0:T(8,128)}, f32[64,384]{1,0:T(8,128)S(1)}, u32[]{:S(2)}) copy-start(f32[64,384]{1,0:T(8,128)S(1)} %maximum_dynamic-update-slice_fusion) | copy-start | bytes 294916
  79.1 9.6 %collective-permute-start.13 = (bf16[64,384]{1,0:T(8,128)(2,1)S(1)}, bf16[64,384]{1,0:T(8,128)(2,1)S(1)}, u32[]{:S(2)}, u32[]{:S(2)}) collective-permute-start(bf16[64,384]{1,0:T(8,128)(2,1)S(1)} %convert.27), channel_id=1, source_target_pairs={{2,0},{4,2},{6,4},{8,6},{10,8},{12,10},{14,12},{16,14},{18,16},{20... | collective-permute-start | bytes 147464 | tf_op jit(solution)/shard_map/ppermute | solution.py:14
  81.0 7.7 %collective-permute-start.12 = (bf16[64,384]{1,0:T(8,128)(2,1)S(1)}, bf16[64,384]{1,0:T(8,128)(2,1)S(1)}, u32[]{:S(2)}, u32[]{:S(2)}) collective-permute-start(bf16[64,384]{1,0:T(8,128)(2,1)S(1)} %convert.27), channel_id=1, source_target_pairs={{0,2},{2,4},{4,6},{6,8},{8,10},{10,12},{12,14},{14,16},{16,18},{18... | collective-permute-start | bytes 147464 | tf_op jit(solution)/shard_map/ppermute | solution.py:14
  95.2 2.5 %copy-start.10 = (pred[96]{0:T(512)(128)(4,1)S(1)}, pred[96]{0:T(512)(128)(4,1)}, u32[]{:S(2)}) copy-start(pred[96]{0:T(512)(128)(4,1)} %get-tuple-element.20) | copy-start | bytes 292
  96.1 3.7 %copy-start.7 = (f32[96,192]{1,0:T(8,128)}, f32[96,192]{1,0:T(8,128)S(1)}, u32[]{:S(2)}) copy-start(f32[96,192]{1,0:T(8,128)S(1)} %gather_fusion.8) | copy-start | bytes 221188
  111.4 1.7 %copy-start.8 = (f32[96,192]{1,0:T(8,128)S(1)}, f32[96,192]{1,0:T(8,128)}, u32[]{:S(2)}) copy-start(f32[96,192]{1,0:T(8,128)} %copy-done.7) | copy-start | bytes 221188
  111.4 1.7 %copy-start.11 = (pred[96]{0:T(512)(128)(4,1)S(1)}, pred[96]{0:T(512)(128)(4,1)}, u32[]{:S(2)}) copy-start(pred[96]{0:T(512)(128)(4,1)} %get-tuple-element.20) | copy-start | bytes 292
  111.5 1.7 %copy-start.17 = (f32[96]{0:T(128)S(1)}, f32[96]{0:T(128)}, u32[]{:S(2)}) copy-start(f32[96]{0:T(128)} %broadcast_add_fusion.1) | copy-start | bytes 1156
  113.2 2.6 %copy-start.13 = (s32[96]{0:T(128)S(1)}, s32[96]{0:T(128)}, u32[]{:S(2)}) copy-start(s32[96]{0:T(128)} %get-tuple-element.21) | copy-start | bytes 1156
  117.4 1.8 %copy-start.2 = (f32[96,2048]{1,0:T(8,128)S(1)}, f32[96,2048]{1,0:T(8,128)}, u32[]{:S(2)}) copy-start(f32[96,2048]{1,0:T(8,128)} %gather_fusion.15) | copy-start | bytes 2359300
  117.4 1.8 %copy-start.3 = (f32[96,2048]{1,0:T(8,128)S(1)}, f32[96,2048]{1,0:T(8,128)}, u32[]{:S(2)}) copy-start(f32[96,2048]{1,0:T(8,128)} %gather_fusion.12) | copy-start | bytes 2359300
  117.4 1.7 %copy-start.16 = (f32[96]{0:T(128)S(1)}, f32[96]{0:T(128)}, u32[]{:S(2)}) copy-start(f32[96]{0:T(128)} %broadcast_add_fusion) | copy-start | bytes 1156
  119.2 3.2 %copy-start.12 = (s32[96]{0:T(128)S(1)}, s32[96]{0:T(128)}, u32[]{:S(2)}) copy-start(s32[96]{0:T(128)} %get-tuple-element.22) | copy-start | bytes 1156
where the time goes:
time: 127 us; the launch traced here: 126 us
  starting transfers between devices  42.9 us (34%)
  local copies, waits for them, and re-layouts  42.8 us (34%)
  matrix products  12.9 us (10%)
  other arithmetic  11.3 us (9%)
  waiting for transfers between devices  6.78 us (5%)
  blocking collectives  6.44 us (5%)
  between operations  2.49 us (2%)
    ppermute x14, starting transfers between devices, from_behind(): return lax.ppermute(block, axis, route)  37.1 us
    ppermute x14, waiting for transfers between devices, from_behind(): return lax.ppermute(block, axis, route)  6.78 us
    all_gather x1, blocking collectives, shards(): all_traces = lax.all_gather(rounded, 'frm', axis=1, tiled=True)  6.44 us
    all_to_all x1, starting transfers between devices, shards(): lax.all_to_all(frames, 'frm', split_axis=0, concat_axis=1, tiled=True)  5.87 us
    dot_general x2, matrix products, shards(): product = jnp.dot(shaped, gram_cols, precision=highest)  5.75 us
    convert_element_type x2, local copies, waits for them, and re-layouts, window_mask(): expanded = jnp.repeat(support, TILE, axis=0).astype(jnp.float32)  5.58 us
    all_to_all x1, local copies, waits for them, and re-layouts, shards(): lax.all_to_all(frames, 'frm', split_axis=0, concat_axis=1, tiled=True)  4.7 us
    convert_element_type x1, other arithmetic, shards(): active = (footprints.astype(jnp.float32) * keep).astype(jnp.bfloat16)  4.39 us
  transfers between devices with their start and end apart: 15, of which 2 were waited for; matrix products, arithmetic and copies ran while one was open for 34% of the time, Pallas kernels for 0%

commit v1 on v0

--- a/solution.py
+++ b/solution.py
@@ -1,3 +1,4 @@
+import functools
 import jax
 import jax.numpy as jnp
 from jax import lax
@@ -6,6 +7,22 @@
 BLOCK = 32
 TILE = 16
 highest = lax.Precision.HIGHEST
+
+
+def trails_balance(vector, d_out, in_dim):
+    found_now = jnp.concatenate(
+        jax.lax.all_to_all(
+            jnp.stack(jnp.split(vector, jax.lax.axis_size("frm"), axis=d_out), axis=0),
+            axis_name="frm",
+            split_axis=0,
+            concat_axis=0,
+        ),
+        axis=in_dim,
+    )
+    return found_now
+
+
+_begin_loops = functools.partial(trails_balance, d_out=0, in_dim=1)
 
 
 def from_behind(block, axis, distance):
@@ -79,7 +96,7 @@
     shares = lax.axis_size("frm")
     share_rows = footprints.shape[0] // shares
     row_begin = lax.axis_index("frm") * share_rows
-    pixel_rows = lax.all_to_all(frames, "frm", split_axis=0, concat_axis=1, tiled=True)
+    pixel_rows = _begin_loops(frames)
     all_traces = lax.all_gather(rounded, "frm", axis=1, tiled=True)
     mixing = jnp.einsum("pt,kt->pk", pixel_rows, all_traces, preferred_element_type=jnp.float32)
     gram = jnp.einsum("kt,jt->kj", all_traces, all_traces, preferred_element_type=jnp.float32)

time: 127 us -> 132 us (1.039)
  other arithmetic: 11.3 us -> 14.8 us
  local copies, waits for them, and re-layouts: 42.8 us -> 44.8 us
    all_to_all x1 -> x0, local copies, waits for them, and re-layouts: 4.7 us -> none  [shards(): lax.all_to_all(frames, 'frm', split_axis=0, concat_axis=1, tiled=True)]
    split x0 -> x1, local copies, waits for them, and re-layouts: none -> 3.39 us  [trails_balance(): jnp.split(vector, jax.lax.axis_size('frm'), axis=d_out)]
    unnamed x45 -> x47, local copies, waits for them, and re-layouts: 3.72 us -> 7.08 us
    another operation x0 -> x1, other arithmetic: none -> 3.34 us  [trails_balance(): jnp.stack(jnp.split(vector, jax.lax.axis_size('frm'), axis=d_out), axis=0)]
  transfers between devices with their start and end apart: 15 -> 15, of which waited for: 2 -> 2; matrix products, arithmetic and copies ran while one was open for 34% -> 40% of each run, Pallas kernels for 0% -> 0%
where the time goes in v1:
time: 132 us; the launch traced here: 131 us
  local copies, waits for them, and re-layouts  44.8 us (34%)
  starting transfers between devices  43 us (33%)
  other arithmetic  14.8 us (11%)
  matrix products  12.9 us (10%)
  waiting for transfers between devices  6.78 us (5%)
  blocking collectives  6.44 us (5%)
  between operations  2.57 us (2%)
    ppermute x14, starting transfers between devices, from_behind(): return lax.ppermute(block, axis, route)  37.1 us
    unnamed x47, local copies, waits for them, and re-layouts  7.08 us
    ppermute x14, waiting for transfers between devices, from_behind(): return lax.ppermute(block, axis, route)  6.78 us
    all_gather x1, blocking collectives, shards(): all_traces = lax.all_gather(rounded, 'frm', axis=1, tiled=True)  6.44 us
    all_to_all x1, starting transfers between devices, trails_balance(): jax.lax.all_to_all(jnp.stack(jnp.split(vector, jax.lax.axis_size('frm'),...  5.93 us
    dot_general x2, matrix products, shards(): product = jnp.dot(shaped, gram_cols, precision=highest)  5.74 us
    convert_element_type x2, local copies, waits for them, and re-layouts, window_mask(): expanded = jnp.repeat(support, TILE, axis=0).astype(jnp.float32)  5.51 us
    convert_element_type x1, other arithmetic, shards(): active = (footprints.astype(jnp.float32) * keep).astype(jnp.bfloat16)  4.37 us
  transfers between devices with their start and end apart: 15, of which 2 were waited for; matrix products, arithmetic and copies ran while one was open for 40% of the time, Pallas kernels for 0%

profile of v1, /device:TPU:10, one launch (start us, length us, event | category | flops | bytes accessed | tf_op | source)
XLA Modules:
  0.0 131.2 jit_solution(2409614321807944653)
XLA Ops:
  0.6 0.9 copy.35
  1.5 2.7 %collective-permute-start.6 = (f32[64,384]{1,0:T(8,128)S(1)}, f32[64,384]{1,0:T(8,128)}, u32[]{:S(2)}, u32[]{:S(2)}) collective-permute-start(f32[64,384]{1,0:T(8,128)S(1)} %copy.35), channel_id=1, source_target_pairs={{2,0},{4,2},{6,4},{8,6},{10,8},{12,10},{14,12},{16,14},{18,16},{20... | collective-permute-start | bytes 294920 | tf_op jit(solution)/shard_map/ppermute | solution.py:31
  4.3 1.9 %collective-permute-start.5 = (f32[64,384]{1,0:T(8,128)S(1)}, f32[64,384]{1,0:T(8,128)}, u32[]{:S(2)}, u32[]{:S(2)}) collective-permute-start(f32[64,384]{1,0:T(8,128)S(1)} %copy.35), channel_id=1, source_target_pairs={{0,2},{2,4},{4,6},{6,8},{8,10},{10,12},{12,14},{14,16},{16,18},{18... | collective-permute-start | bytes 294920 | tf_op jit(solution)/shard_map/ppermute | solution.py:31
  6.2 3.1 %collective-permute-start.4 = (f32[64,384]{1,0:T(8,128)S(1)}, f32[64,384]{1,0:T(8,128)}, u32[]{:S(2)}, u32[]{:S(2)}) collective-permute-start(f32[64,384]{1,0:T(8,128)S(1)} %copy.35), channel_id=1, source_target_pairs={{0,4},{2,6},{4,8},{6,10},{8,12},{10,14},{12,16},{14,18},{16,20},{1... | collective-permute-start | bytes 294920 | tf_op jit(solution)/shard_map/ppermute | solution.py:31
  9.3 3.4 %fusion.28 = (bf16[2048,384]{1,0:T(8,128)(2,1)}, bf16[2048,384]{1,0:T(8,128)(2,1)S(1)}) fusion(bf16[4096,384]{1,0:T(8,128)(2,1)} %param.11), kind=kLoop, calls=%fused_computation.96 | loop fusion | bytes 6291456 | tf_op jit(solution)/shard_map/split | solution.py:15
  12.7 1.7 %copy.20 = bf16[2048,384]{0,1:T(8,128)(2,1)S(1)} copy(bf16[2048,384]{1,0:T(8,128)(2,1)} %get-tuple-element.7) | data formatting | bytes 3145728
  14.4 1.7 %copy.21 = bf16[2048,384]{0,1:T(8,128)(2,1)} copy(bf16[2048,384]{1,0:T(8,128)(2,1)S(1)} %get-tuple-element.8) | data formatting | bytes 3145728
  16.1 3.3 %pad_maximum_fusion = bf16[2,2048,384]{1,2,0:T(8,128)(2,1)} fusion(bf16[1,2048,384]{1,2,0:T(8,128)(2,1)} %bitcast.57, bf16[1,2048,384]{1,2,0:T(8,128)(2,1)S(1)} %bitcast.56), kind=kLoop, calls=%fused_computation.18 | loop fusion | flops 1572864 | bytes 6291456 | tf_op jit(solution)/shard_map/stack | solution.py:15
  19.4 5.9 %all-to-all-start = ((bf16[2,2048,384]{1,2,0:T(8,128)(2,1)}), bf16[2,2048,384]{1,2,0:T(8,128)(2,1)}, u32[]{:S(2)}, u32[]{:S(2)}) async-start(bf16[2,2048,384]{1,2,0:T(8,128)(2,1)} %pad_maximum_fusion), calls=%async_computation | async-start | bytes 6291456 | tf_op jit(solution)/shard_map/all_to_all | solution.py:14
  25.5 2.3 %broadcast_in_dim.69 = f32[256,16,192]{2,1,0:T(8,128)} broadcast(f32[256,192]{1,0:T(8,128)S(1)} %copy.11), dimensions={0,2} | broadcast | bytes 3342336 | tf_op jit(solution)/shard_map/broadcast_in_dim | solution.py:35
  27.8 5.4 %copy.12 = f32[4096,192]{0,1:T(8,128)} copy(f32[4096,192]{1,0:T(8,128)} %bitcast.55) | data formatting | bytes 6291456 | tf_op jit(solution)/shard_map/convert_element_type | solution.py:35
  33.2 4.4 %multiply_convert_fusion = (bf16[4096,192]{0,1:T(8,128)(2,1)S(1)}, f32[4096,192]{0,1:T(8,128)}) fusion(bf16[4096,192]{0,1:T(8,128)(2,1)S(1)} %copy-done.5, f32[4096,192]{0,1:T(8,128)} %copy.12, f32[192]{0:T(256)S(1)} %select_convert_fusion), kind=kLoop, calls=%fused_computation.19 | loop fusion | flops 3145728 | bytes 9437952 | tf_op jit(solution)/shard_map/convert_element_type | solution.py:67
  37.6 0.6 fusion.34
  38.2 0.7 fusion.30
  38.8 3.3 %collective-permute-start.3 = (f32[64,192]{1,0:T(8,128)}, f32[64,192]{1,0:T(8,128)}, u32[]{:S(2)}, u32[]{:S(2)}) collective-permute-start(f32[64,192]{1,0:T(8,128)} %get-tuple-element.12), channel_id=1, source_target_pairs={{0,2},{2,4},{4,6},{6,8},{8,10},{10,12},{12,14},{14,16},{16,18},{18... | collective-permute-start | bytes 147464 | tf_op jit(solution)/shard_map/ppermute | solution.py:31
  42.2 3.1 %collective-permute-start.2 = (f32[64,192]{1,0:T(8,128)}, f32[64,192]{1,0:T(8,128)}, u32[]{:S(2)}, u32[]{:S(2)}) collective-permute-start(f32[64,192]{1,0:T(8,128)} %get-tuple-element.13), channel_id=1, source_target_pairs={{2,0},{4,2},{6,4},{8,6},{10,8},{12,10},{14,12},{16,14},{18,16},{20... | collective-permute-start | bytes 147464 | tf_op jit(solution)/shard_map/ppermute | solution.py:31
  45.4 0.7 gather_fusion.4
  46.3 0.7 gather_fusion
  47.2 0.6 compare_select_fusion
  48.3 0.5 compare_and_fusion
  48.8 2.9 %fusion.33 = f32[192,384]{1,0:T(8,128)S(1)} fusion(bf16[4096,192]{0,1:T(8,128)(2,1)S(1)} %get-tuple-element.4, bf16[4096,384]{1,0:T(8,128)(2,1)} %param.11), kind=kOutput, calls=%fused_computation.101 | convolution fusion | flops 603979776 | bytes 5013504 | tf_op jit(solution)/shard_map/pk,pt->kt/dot_general | solution.py:68
  51.9 1.5 %constant_dynamic-slice_fusion.1 = f32[2048,192]{0,1:T(8,128)S(1)} fusion(f32[4096,192]{0,1:T(8,128)} %get-tuple-element.6, s32[]{:T(128)S(6)} %select_n.126), kind=kLoop, calls=%fused_computation.70 | loop fusion | bytes 3145732 | tf_op jit(solution)/shard_map/dynamic_slice | solution.py:104
  53.5 0.7 fusion.29
  54.1 0.6 fusion.25
  54.8 0.7 constant_dynamic-slice_fusion.2
  56.8 2.8 %collective-permute-start.7 = (f32[64,384]{1,0:T(8,128)S(1)}, f32[64,384]{1,0:T(8,128)S(1)}, u32[]{:S(2)}, u32[]{:S(2)}) collective-permute-start(f32[64,384]{1,0:T(8,128)S(1)} %copy.35), channel_id=1, source_target_pairs={{4,0},{6,2},{8,4},{10,6},{12,8},{14,10},{16,12},{18,14},{20,16},{2... | collective-permute-start | bytes 294920 | tf_op jit(solution)/shard_map/ppermute | solution.py:31
  59.6 2.7 %collective-permute-start = (f32[64,384]{1,0:T(8,128)}, f32[64,384]{1,0:T(8,128)}, u32[]{:S(2)}, u32[]{:S(2)}) collective-permute-start(f32[64,384]{1,0:T(8,128)} %get-tuple-element.9), channel_id=1, source_target_pairs={{2,0},{4,2},{6,4},{8,6},{10,8},{12,10},{14,12},{16,14},{18,16},{20... | collective-permute-start | bytes 294920 | tf_op jit(solution)/shard_map/ppermute | solution.py:31
  62.3 1.0 pad_add_fusion
  63.4 0.7 gather_fusion.1
  64.2 0.7 gather_fusion.2
  64.9 1.9 %collective-permute-start.1 = (f32[64,384]{1,0:T(8,128)}, f32[64,384]{1,0:T(8,128)S(1)}, u32[]{:S(2)}, u32[]{:S(2)}) collective-permute-start(f32[64,384]{1,0:T(8,128)} %get-tuple-element.10), channel_id=1, source_target_pairs={{0,2},{2,4},{4,6},{6,8},{8,10},{10,12},{12,14},{14,16},{16,18},{18... | collective-permute-start | bytes 294920 | tf_op jit(solution)/shard_map/ppermute | solution.py:31
  66.8 0.9 constant_dynamic-update-slice_fusion.4
  67.7 0.9 constant_dynamic-update-slice_fusion.3
  68.6 0.9 constant_dynamic-update-slice_fusion.1
  69.6 2.4 %collective-permute-done.1 = f32[64,384]{1,0:T(8,128)S(1)} collective-permute-done((f32[64,384]{1,0:T(8,128)}, f32[64,384]{1,0:T(8,128)S(1)}, u32[]{:S(2)}, u32[]{:S(2)}) %collective-permute-start.1) | collective-permute-done | bytes 98336 | tf_op jit(solution)/shard_map/ppermute | solution.py:31
  71.9 1.0 fusion.11
  73.3 1.9 %collective-permute-start.8 = (f32[64,384]{1,0:T(8,128)S(1)}, f32[64,384]{1,0:T(8,128)S(1)}, u32[]{:S(2)}, u32[]{:S(2)}) collective-permute-start(f32[64,384]{1,0:T(8,128)S(1)} %maximum_dynamic-update-slice_fusion.1), channel_id=1, source_target_pairs={{0,4},{2,6},{4,8},{6,10},{8,12},{10,14},{12,16},{14,18},{16,20},{1... | collective-permute-start | bytes 294920 | tf_op jit(solution)/shard_map/ppermute | solution.py:31
  75.2 4.8 %collective-permute-start.11 = (f32[64,384]{1,0:T(8,128)S(1)}, f32[64,384]{1,0:T(8,128)S(1)}, u32[]{:S(2)}, u32[]{:S(2)}) collective-permute-start(f32[64,384]{1,0:T(8,128)S(1)} %maximum_dynamic-update-slice_fusion.1), channel_id=1, source_target_pairs={{4,0},{6,2},{8,4},{10,6},{12,8},{14,10},{16,12},{18,14},{20,16},{2... | collective-permute-start | bytes 294920 | tf_op jit(solution)/shard_map/ppermute | solution.py:31
  80.0 1.9 %collective-permute-start.10 = (f32[64,384]{1,0:T(8,128)S(1)}, f32[64,384]{1,0:T(8,128)S(1)}, u32[]{:S(2)}, u32[]{:S(2)}) collective-permute-start(f32[64,384]{1,0:T(8,128)S(1)} %maximum_dynamic-update-slice_fusion.1), channel_id=1, source_target_pairs={{2,0},{4,2},{6,4},{8,6},{10,8},{12,10},{14,12},{16,14},{18,16},{20... | collective-permute-start | bytes 294920 | tf_op jit(solution)/shard_map/ppermute | solution.py:31
  82.0 2.4 %collective-permute-start.9 = (f32[64,384]{1,0:T(8,128)S(1)}, f32[64,384]{1,0:T(8,128)S(1)}, u32[]{:S(2)}, u32[]{:S(2)}) collective-permute-start(f32[64,384]{1,0:T(8,128)S(1)} %maximum_dynamic-update-slice_fusion.1), channel_id=1, source_target_pairs={{0,2},{2,4},{4,6},{6,8},{8,10},{10,12},{12,14},{14,16},{16,18},{18... | collective-permute-start | bytes 294920 | tf_op jit(solution)/shard_map/ppermute | solution.py:31
  84.4 4.4 %collective-permute-done.9 = f32[64,384]{1,0:T(8,128)S(1)} collective-permute-done((f32[64,384]{1,0:T(8,128)S(1)}, f32[64,384]{1,0:T(8,128)S(1)}, u32[]{:S(2)}, u32[]{:S(2)}) %collective-permute-start.9) | collective-permute-done | bytes 98336 | tf_op jit(solution)/shard_map/ppermute | solution.py:31
  89.3 1.9 %collective-permute-start.13 = (bf16[64,384]{1,0:T(8,128)(2,1)S(1)}, bf16[64,384]{1,0:T(8,128)(2,1)S(1)}, u32[]{:S(2)}, u32[]{:S(2)}) collective-permute-start(bf16[64,384]{1,0:T(8,128)(2,1)S(1)} %convert.27), channel_id=1, source_target_pairs={{2,0},{4,2},{6,4},{8,6},{10,8},{12,10},{14,12},{16,14},{18,16},{20... | collective-permute-start | bytes 147464 | tf_op jit(solution)/shard_map/ppermute | solution.py:31
  91.2 2.4 %collective-permute-start.12 = (bf16[64,384]{1,0:T(8,128)(2,1)S(1)}, bf16[64,384]{1,0:T(8,128)(2,1)S(1)}, u32[]{:S(2)}, u32[]{:S(2)}) collective-permute-start(bf16[64,384]{1,0:T(8,128)(2,1)S(1)} %convert.27), channel_id=1, source_target_pairs={{0,2},{2,4},{4,6},{6,8},{8,10},{10,12},{12,14},{14,16},{16,18},{18... | collective-permute-start | bytes 147464 | tf_op jit(solution)/shard_map/ppermute | solution.py:31
  93.7 1.7 %gather_fusion.15 = f32[96,2048]{1,0:T(8,128)} fusion(f32[2048,192]{0,1:T(8,128)S(1)} %constant_dynamic-slice_fusion.1, s32[1024]{0:T(1024)S(1)} %get-tuple-element.25), kind=kCustom, calls=%fused_computation.7.clone | custom fusion | bytes 1573248 | tf_op jit(solution)/shard_map/jit(_take)/gather | solution.py:117
  95.4 1.7 %gather_fusion.10 = f32[96,2048]{1,0:T(8,128)} fusion(f32[2048,192]{0,1:T(8,128)S(1)} %constant_dynamic-slice_fusion.1, s32[1024]{0:T(1024)S(1)} %get-tuple-element.26), kind=kCustom, calls=%fused_computation.4.clone | custom fusion | bytes 1573248 | tf_op jit(solution)/shard_map/jit(_take)/gather | solution.py:117
  97.1 1.7 %gather_fusion.6 = f32[96,2048]{1,0:T(8,128)} fusion(f32[2048,192]{0,1:T(8,128)S(1)} %dynamic-slice_convert_fusion, s32[1024]{0:T(1024)S(1)} %get-tuple-element.26), kind=kCustom, calls=%fused_computation.clone | custom fusion | bytes 1573248 | tf_op jit(solution)/shard_map/jit(_take)/gather | solution.py:115
  98.9 6.4 %all_gather.3 = bf16[192,768]{1,0:T(8,128)(2,1)S(1)} all-gather(bf16[192,384]{1,0:T(8,128)(2,1)S(1)} %pad_maximum_fusion.1), channel_id=1, replica_groups=mesh['pix'=16,'frm'=2] {'frm'}, dimensions={1}, use_global_device_ids=true | all-gather | bytes 442368 | tf_op jit(solution)/shard_map/all_gather | solution.py:100
  105.6 0.7 gather_fusion.8
  106.3 0.7 gather_fusion.13
  107.2 0.6 gather_fusion.14
  108.0 0.6 gather_fusion.9
  108.7 1.2 gather_fusion.5
  110.1 1.2 gather_fusion.3
  111.3 0.5 broadcast_add_fusion
  111.8 0.6 broadcast_add_fusion.1
  112.4 2.7 %fusion.36 = f32[2048,192]{0,1:T(8,128)S(1)} fusion(bf16[192,768]{1,0:T(8,128)(2,1)S(1)} %all_gather.3, bf16[2048,768]{0,1:T(8,128)(2,1)} %bitcast.7), kind=kOutput, calls=%fused_computation.104 | convolution fusion | flops 603979776 | bytes 5013504 | tf_op jit(solution)/shard_map/pt,kt->pk/dot_general | solution.py:101
  115.1 1.7 %gather_fusion.12 = f32[96,2048]{1,0:T(8,128)} fusion(f32[2048,192]{0,1:T(8,128)S(1)} %fusion.36, s32[1024]{0:T(1024)S(1)} %get-tuple-element.25), kind=kCustom, calls=%fused_computation.6.clone | custom fusion | bytes 1573248 | tf_op jit(solution)/shard_map/jit(_take)/gather | solution.py:116
  116.9 1.7 %gather_fusion.7 = f32[96,2048]{1,0:T(8,128)} fusion(f32[2048,192]{0,1:T(8,128)S(1)} %fusion.36, s32[1024]{0:T(1024)S(1)} %get-tuple-element.26), kind=kCustom, calls=%fused_computation.3.clone | custom fusion | bytes 1573248 | tf_op jit(solution)/shard_map/jit(_take)/gather | solution.py:116
  118.6 2.5 %fusion.9 = f32[96,2048]{1,0:T(8,128)S(1)} fusion(f32[96,2048]{1,0:T(8,128)} %gather_fusion.10, f32[96,2048]{1,0:T(8,128)} %gather_fusion.7, f32[96,2048]{1,0:T(8,128)} %gather_fusion.6, bf16[4096,192]{0,1:T(8,128)(2,1)} %copy-done.1, s32[]{:T(128)S(6)} %select_n.126, f32[96]{0:T(128)S(1)} %copy-done.17, pred[96]{0:T(512)(128)(4,1)S(1)} %copy-done.11, ...), kind=kOutput, calls=%fused_computation.31 | convolution fusion | flops 454576128 | bytes 4032004 | tf_op jit(solution)/shard_map/dot_general | solution.py:118
  121.2 1.8 %scatter_fusion = f32[2048,192]{0,1:T(8,128)S(1)} fusion(f32[2048,192]{0,1:T(8,128)S(1)} %dynamic-slice_convert_fusion, s32[96]{0:T(128)S(1)} %copy-done.13, f32[96,2048]{1,0:T(8,128)S(1)} %fusion.9), kind=kCustom, calls=%fused_computation.16 | custom fusion | bytes 2359680 | tf_op jit(solution)/shard_map/scatter | solution.py:122
  123.0 1.7 %gather_fusion.11 = f32[96,2048]{1,0:T(8,128)} fusion(f32[2048,192]{0,1:T(8,128)S(1)} %scatter_fusion, s32[1024]{0:T(1024)S(1)} %get-tuple-element.25), kind=kCustom, calls=%fused_computation.5.clone | custom fusion | bytes 1573248 | tf_op jit(solution)/shard_map/jit(_take)/gather | solution.py:115
  124.8 3.2 %fusion.5 = f32[96,2048]{1,0:T(8,128)} fusion(f32[2048,192]{0,1:T(8,128)S(1)} %scatter_fusion, f32[96,2048]{1,0:T(8,128)S(1)} %copy-done.2, f32[96,2048]{1,0:T(8,128)S(1)} %copy-done.3, f32[96,2048]{1,0:T(8,128)} %gather_fusion.11, f32[96]{0:T(128)S(1)} %copy-done.16, pred[96]{0:T(512)(128)(4,1)S(1)} %get-tuple-element.21, f32[96,192]{1,0:T(8,128)S(1)} %gather_fusion.13), kind=kOutput, calls=%fused_computation.27 | convolution fusion | flops 454576128 | bytes 4792800 | tf_op jit(solution)/shard_map/dot_general | solution.py:118
  128.0 2.2 %scatter_fusion.1 = f32[2048,192]{0,1:T(8,128)S(1)} fusion(f32[2048,192]{0,1:T(8,128)S(1)} %scatter_fusion, s32[96]{0:T(128)S(1)} %copy-done.12, f32[96,2048]{1,0:T(8,128)} %fusion.5), kind=kCustom, calls=%fused_computation.17 | custom fusion | bytes 2359680 | tf_op jit(solution)/shard_map/scatter | solution.py:122
  130.2 1.0 convert_element_type.39
  (88 shorter events, 3.2 us)
Async XLA Ops:
  1.5 67.1 %collective-permute-start.6 = (f32[64,384]{1,0:T(8,128)S(1)}, f32[64,384]{1,0:T(8,128)}, u32[]{:S(2)}, u32[]{:S(2)}) collective-permute-start(f32[64,384]{1,0:T(8,128)S(1)} %copy.35), channel_id=1, source_target_pairs={{2,0},{4,2},{6,4},{8,6},{10,8},{12,10},{14,12},{16,14},{18,16},{20... | collective-permute-start | bytes 294920 | tf_op jit(solution)/shard_map/ppermute | solution.py:31
  4.3 63.4 %collective-permute-start.5 = (f32[64,384]{1,0:T(8,128)S(1)}, f32[64,384]{1,0:T(8,128)}, u32[]{:S(2)}, u32[]{:S(2)}) collective-permute-start(f32[64,384]{1,0:T(8,128)S(1)} %copy.35), channel_id=1, source_target_pairs={{0,2},{2,4},{4,6},{6,8},{8,10},{10,12},{12,14},{14,16},{16,18},{18... | collective-permute-start | bytes 294920 | tf_op jit(solution)/shard_map/ppermute | solution.py:31
  6.2 58.7 %collective-permute-start.4 = (f32[64,384]{1,0:T(8,128)S(1)}, f32[64,384]{1,0:T(8,128)}, u32[]{:S(2)}, u32[]{:S(2)}) collective-permute-start(f32[64,384]{1,0:T(8,128)S(1)} %copy.35), channel_id=1, source_target_pairs={{0,4},{2,6},{4,8},{6,10},{8,12},{10,14},{12,16},{14,18},{16,20},{1... | collective-permute-start | bytes 294920 | tf_op jit(solution)/shard_map/ppermute | solution.py:31
  19.4 5.9 %copy-start.9 = (s32[256,192]{0,1:T(8,128)S(1)}, s32[256,192]{0,1:T(8,128)}, u32[]{:S(2)}) copy-start(s32[256,192]{0,1:T(8,128)} %param.13) | copy-start | bytes 589828
  19.4 93.0 %all-to-all-start = ((bf16[2,2048,384]{1,2,0:T(8,128)(2,1)}), bf16[2,2048,384]{1,2,0:T(8,128)(2,1)}, u32[]{:S(2)}, u32[]{:S(2)}) async-start(bf16[2,2048,384]{1,2,0:T(8,128)(2,1)} %pad_maximum_fusion), calls=%async_computation | async-start | bytes 6291456 | tf_op jit(solution)/shard_map/all_to_all | solution.py:14
  27.8 5.4 %copy-start.5 = (bf16[4096,192]{0,1:T(8,128)(2,1)S(1)}, bf16[4096,192]{0,1:T(8,128)(2,1)}, u32[]{:S(2)}) copy-start(bf16[4096,192]{0,1:T(8,128)(2,1)} %param.12) | copy-start | bytes 4718596
  37.6 14.2 %copy-start.1 = (bf16[4096,192]{0,1:T(8,128)(2,1)}, bf16[4096,192]{0,1:T(8,128)(2,1)S(1)}, u32[]{:S(2)}) copy-start(bf16[4096,192]{0,1:T(8,128)(2,1)S(1)} %get-tuple-element.4) | copy-start | bytes 4718596
  37.6 7.8 %copy-start = (s32[16,2]{0,1:T(2,128)S(1)}, s32[16,2]{0,1:T(2,128)}, u32[]{:S(2)}) copy-start(s32[16,2]{0,1:T(2,128)} %param.15) | copy-start | bytes 388
  38.8 17.9 %collective-permute-start.3 = (f32[64,192]{1,0:T(8,128)}, f32[64,192]{1,0:T(8,128)}, u32[]{:S(2)}, u32[]{:S(2)}) collective-permute-start(f32[64,192]{1,0:T(8,128)} %get-tuple-element.12), channel_id=1, source_target_pairs={{0,2},{2,4},{4,6},{6,8},{8,10},{10,12},{12,14},{14,16},{16,18},{18... | collective-permute-start | bytes 147464 | tf_op jit(solution)/shard_map/ppermute | solution.py:31
  42.2 17.4 %collective-permute-start.2 = (f32[64,192]{1,0:T(8,128)}, f32[64,192]{1,0:T(8,128)}, u32[]{:S(2)}, u32[]{:S(2)}) collective-permute-start(f32[64,192]{1,0:T(8,128)} %get-tuple-element.13), channel_id=1, source_target_pairs={{2,0},{4,2},{6,4},{8,6},{10,8},{12,10},{14,12},{16,14},{18,16},{20... | collective-permute-start | bytes 147464 | tf_op jit(solution)/shard_map/ppermute | solution.py:31
  51.7 1.7 %copy-start.6 = (f32[192,384]{1,0:T(8,128)}, f32[192,384]{1,0:T(8,128)S(1)}, u32[]{:S(2)}) copy-start(f32[192,384]{1,0:T(8,128)S(1)} %fusion.33) | copy-start | bytes 884740
  51.9 2.8 %copy-start.14 = (s32[96]{0:T(128)S(1)}, s32[96]{0:T(128)}, u32[]{:S(2)}) copy-start(s32[96]{0:T(128)} %compare_select_fusion) | copy-start | bytes 1156
  51.9 2.8 %copy-start.15 = (s32[96]{0:T(128)S(1)}, s32[96]{0:T(128)}, u32[]{:S(2)}) copy-start(s32[96]{0:T(128)} %compare_select_fusion.1) | copy-start | bytes 1156
  56.8 12.8 %collective-permute-start.7 = (f32[64,384]{1,0:T(8,128)S(1)}, f32[64,384]{1,0:T(8,128)S(1)}, u32[]{:S(2)}, u32[]{:S(2)}) collective-permute-start(f32[64,384]{1,0:T(8,128)S(1)} %copy.35), channel_id=1, source_target_pairs={{4,0},{6,2},{8,4},{10,6},{12,8},{14,10},{16,12},{18,14},{20,16},{2... | collective-permute-start | bytes 294920 | tf_op jit(solution)/shard_map/ppermute | solution.py:31
  59.6 9.9 %collective-permute-start = (f32[64,384]{1,0:T(8,128)}, f32[64,384]{1,0:T(8,128)}, u32[]{:S(2)}, u32[]{:S(2)}) collective-permute-start(f32[64,384]{1,0:T(8,128)} %get-tuple-element.9), channel_id=1, source_target_pairs={{2,0},{4,2},{6,4},{8,6},{10,8},{12,10},{14,12},{16,14},{18,16},{20... | collective-permute-start | bytes 294920 | tf_op jit(solution)/shard_map/ppermute | solution.py:31
  64.9 7.0 %collective-permute-start.1 = (f32[64,384]{1,0:T(8,128)}, f32[64,384]{1,0:T(8,128)S(1)}, u32[]{:S(2)}, u32[]{:S(2)}) collective-permute-start(f32[64,384]{1,0:T(8,128)} %get-tuple-element.10), channel_id=1, source_target_pairs={{0,2},{2,4},{4,6},{6,8},{8,10},{10,12},{12,14},{14,16},{16,18},{18... | collective-permute-start | bytes 294920 | tf_op jit(solution)/shard_map/ppermute | solution.py:31
  73.3 11.1 %collective-permute-start.8 = (f32[64,384]{1,0:T(8,128)S(1)}, f32[64,384]{1,0:T(8,128)S(1)}, u32[]{:S(2)}, u32[]{:S(2)}) collective-permute-start(f32[64,384]{1,0:T(8,128)S(1)} %maximum_dynamic-update-slice_fusion.1), channel_id=1, source_target_pairs={{0,4},{2,6},{4,8},{6,10},{8,12},{10,14},{12,16},{14,18},{16,20},{1... | collective-permute-start | bytes 294920 | tf_op jit(solution)/shard_map/ppermute | solution.py:31
  75.2 13.7 %collective-permute-start.11 = (f32[64,384]{1,0:T(8,128)S(1)}, f32[64,384]{1,0:T(8,128)S(1)}, u32[]{:S(2)}, u32[]{:S(2)}) collective-permute-start(f32[64,384]{1,0:T(8,128)S(1)} %maximum_dynamic-update-slice_fusion.1), channel_id=1, source_target_pairs={{4,0},{6,2},{8,4},{10,6},{12,8},{14,10},{16,12},{18,14},{20,16},{2... | collective-permute-start | bytes 294920 | tf_op jit(solution)/shard_map/ppermute | solution.py:31
  80.0 8.8 %collective-permute-start.10 = (f32[64,384]{1,0:T(8,128)S(1)}, f32[64,384]{1,0:T(8,128)S(1)}, u32[]{:S(2)}, u32[]{:S(2)}) collective-permute-start(f32[64,384]{1,0:T(8,128)S(1)} %maximum_dynamic-update-slice_fusion.1), channel_id=1, source_target_pairs={{2,0},{4,2},{6,4},{8,6},{10,8},{12,10},{14,12},{16,14},{18,16},{20... | collective-permute-start | bytes 294920 | tf_op jit(solution)/shard_map/ppermute | solution.py:31
  82.0 6.8 %collective-permute-start.9 = (f32[64,384]{1,0:T(8,128)S(1)}, f32[64,384]{1,0:T(8,128)S(1)}, u32[]{:S(2)}, u32[]{:S(2)}) collective-permute-start(f32[64,384]{1,0:T(8,128)S(1)} %maximum_dynamic-update-slice_fusion.1), channel_id=1, source_target_pairs={{0,2},{2,4},{4,6},{6,8},{8,10},{10,12},{12,14},{14,16},{16,18},{18... | collective-permute-start | bytes 294920 | tf_op jit(solution)/shard_map/ppermute | solution.py:31
  89.3 6.1 %copy-start.4 = (f32[64,384]{1,0:T(8,128)}, f32[64,384]{1,0:T(8,128)S(1)}, u32[]{:S(2)}) copy-start(f32[64,384]{1,0:T(8,128)S(1)} %maximum_dynamic-update-slice_fusion) | copy-start | bytes 294916
  89.3 9.5 %collective-permute-start.13 = (bf16[64,384]{1,0:T(8,128)(2,1)S(1)}, bf16[64,384]{1,0:T(8,128)(2,1)S(1)}, u32[]{:S(2)}, u32[]{:S(2)}) collective-permute-start(bf16[64,384]{1,0:T(8,128)(2,1)S(1)} %convert.27), channel_id=1, source_target_pairs={{2,0},{4,2},{6,4},{8,6},{10,8},{12,10},{14,12},{16,14},{18,16},{20... | collective-permute-start | bytes 147464 | tf_op jit(solution)/shard_map/ppermute | solution.py:31
  91.2 7.6 %collective-permute-start.12 = (bf16[64,384]{1,0:T(8,128)(2,1)S(1)}, bf16[64,384]{1,0:T(8,128)(2,1)S(1)}, u32[]{:S(2)}, u32[]{:S(2)}) collective-permute-start(bf16[64,384]{1,0:T(8,128)(2,1)S(1)} %convert.27), channel_id=1, source_target_pairs={{0,2},{2,4},{4,6},{6,8},{8,10},{10,12},{12,14},{14,16},{16,18},{18... | collective-permute-start | bytes 147464 | tf_op jit(solution)/shard_map/ppermute | solution.py:31
  105.3 2.5 %copy-start.10 = (pred[96]{0:T(512)(128)(4,1)S(1)}, pred[96]{0:T(512)(128)(4,1)}, u32[]{:S(2)}) copy-start(pred[96]{0:T(512)(128)(4,1)} %get-tuple-element.22) | copy-start | bytes 292
  106.3 3.7 %copy-start.7 = (f32[96,192]{1,0:T(8,128)}, f32[96,192]{1,0:T(8,128)S(1)}, u32[]{:S(2)}) copy-start(f32[96,192]{1,0:T(8,128)S(1)} %gather_fusion.8) | copy-start | bytes 221188
  116.9 1.7 %copy-start.8 = (f32[96,192]{1,0:T(8,128)S(1)}, f32[96,192]{1,0:T(8,128)}, u32[]{:S(2)}) copy-start(f32[96,192]{1,0:T(8,128)} %copy-done.7) | copy-start | bytes 221188
  116.9 1.7 %copy-start.11 = (pred[96]{0:T(512)(128)(4,1)S(1)}, pred[96]{0:T(512)(128)(4,1)}, u32[]{:S(2)}) copy-start(pred[96]{0:T(512)(128)(4,1)} %get-tuple-element.22) | copy-start | bytes 292
  116.9 1.7 %copy-start.17 = (f32[96]{0:T(128)S(1)}, f32[96]{0:T(128)}, u32[]{:S(2)}) copy-start(f32[96]{0:T(128)} %broadcast_add_fusion.1) | copy-start | bytes 1156
  118.6 2.5 %copy-start.13 = (s32[96]{0:T(128)S(1)}, s32[96]{0:T(128)}, u32[]{:S(2)}) copy-start(s32[96]{0:T(128)} %get-tuple-element.23) | copy-start | bytes 1156
  123.0 1.8 %copy-start.2 = (f32[96,2048]{1,0:T(8,128)S(1)}, f32[96,2048]{1,0:T(8,128)}, u32[]{:S(2)}) copy-start(f32[96,2048]{1,0:T(8,128)} %gather_fusion.15) | copy-start | bytes 2359300
  123.0 1.8 %copy-start.3 = (f32[96,2048]{1,0:T(8,128)S(1)}, f32[96,2048]{1,0:T(8,128)}, u32[]{:S(2)}) copy-start(f32[96,2048]{1,0:T(8,128)} %gather_fusion.12) | copy-start | bytes 2359300
  123.0 1.7 %copy-start.16 = (f32[96]{0:T(128)S(1)}, f32[96]{0:T(128)}, u32[]{:S(2)}) copy-start(f32[96]{0:T(128)} %broadcast_add_fusion) | copy-start | bytes 1156
  124.8 3.2 %copy-start.12 = (s32[96]{0:T(128)S(1)}, s32[96]{0:T(128)}, u32[]{:S(2)}) copy-start(s32[96]{0:T(128)} %get-tuple-element.24) | copy-start | bytes 1156
